TPU v7x, 32 devices: a whole 2x2x4 slice. The times are simulated.
32 devices in a mesh: field: 4 (over y, x), azim: 8 (over z, core).
Axes of the slice: x: 2, y: 2, z: 4, core: 2. Of those that a mesh axis runs over, the one named last changes fastest.
Arguments:
- scalars: float32 [64, 10, 128, 1024], P('field', None, 'azim'), may hold values from -5 to 5
- wiener: float32 [64, 128, 1024], P('field', 'azim'), may hold values from -1.2 to 1.2
- velocity: float32 [128, 1024], P('azim', 'field'), may hold values from 0.5 to 2
- diffusivity: float32 [128, 1024], P('azim', 'field'), may hold values from 0.1 to 0.8
- mix_rate: float32 [128, 1024], P('azim', 'field'), may hold values from 0.5 to 4
- reaction_rate: float32 [10], replicated, may hold values from 0.2 to 1.5
- equilibrium: float32 [10], replicated, may hold values from -3 to 3
Outputs:
- advanced: float32 [64, 10, 128, 1024], P('field', None, 'azim')
- density: float32 [128, 1024], P('azim', 'field')
All inputs are finite; a program needn't handle non-finite values.
Results may differ from a plain program's by a relative error of at most 0.00002.
Values sent between devices are 32-bit elements; how exact they have to be, the bound alone decides.
No kernel may reach another device: no remote copies, remote signals or barrier semaphores. Data moves between devices by JAX's collectives and lax.ppermute only.
A program may use at most 128 MiB of HBM per device.

v0:
```python
import jax
import jax.numpy as jnp
from jax import lax
from jax.sharding import PartitionSpec as P

NF = 64


step_size = 0.2


def with_halo(block, sides, width):
    for axis, dim in sides:
        count = lax.axis_size(axis)
        forward = [(i, i + 1) for i in range(count - 1)]
        forward.append((count - 1, 0))
        backward = [(target, source) for source, target in forward]
        low = lax.ppermute(
            lax.slice_in_dim(block, block.shape[dim] - width, None, axis=dim), axis, forward
        )
        high = lax.ppermute(lax.slice_in_dim(block, 0, width, axis=dim), axis, backward)
        block = jnp.concatenate([low, block, high], axis=dim)
    return block


def advance(
    middle,
    upper_row,
    lower_row,
    velocity,
    diffusivity,
    mix_rate,
    wiener,
    average,
    reaction_rate,
    equilibrium,
):
    gradient = 0.5 * (upper_row - lower_row)
    laplacian = upper_row - 2.0 * middle + lower_row
    heating = 1.0 + 0.5 * middle[:, 0] * middle[:, 0]
    burning = jnp.exp(1.0 - 1.0 / heating)
    source = (
        reaction_rate[None, :, None, None]
        * burning[:, None]
        * (equilibrium[None, :, None, None] - middle)
    )
    tendency = (
        -velocity * gradient
        + diffusivity * laplacian
        - 0.5 * mix_rate * (middle - average)
        + source
    )
    return middle + step_size * tendency + jnp.sqrt(2.0 * diffusivity) * gradient * wiener[:, None]


def field_average(local_sum):
    return lax.psum(local_sum, "field") / NF


def rim_segment(state, gas_state, wiener, reaction_rate, equilibrium):
    padded = with_halo(state, (("azim", 2),), 1)
    average = field_average(jnp.sum(state, axis=0))
    return advance(
        state,
        padded[:, :, 2:],
        padded[:, :, :-2],
        gas_state[0],
        gas_state[1],
        gas_state[2],
        wiener,
        average,
        reaction_rate,
        equilibrium,
    )


def shards(scalars, wiener, velocity, diffusivity, mix_rate, reaction_rate, equilibrium):
    gas_state = (
        lax.all_gather(velocity, "field", axis=1, tiled=True),
        lax.all_gather(diffusivity, "field", axis=1, tiled=True),
        lax.all_gather(mix_rate, "field", axis=1, tiled=True),
    )
    segment_one = rim_segment(scalars, gas_state, wiener, reaction_rate, equilibrium)
    segment_two = rim_segment(segment_one, gas_state, wiener, reaction_rate, equilibrium)
    advanced = 0.5 * scalars + 0.5 * segment_two
    heating = 1.0 + 0.5 * advanced[:, 0] * advanced[:, 0]
    totals = lax.psum_scatter(jnp.sum(heating, axis=0), "field", scatter_dimension=1, tiled=True)
    density = 1.0 / (totals / NF)
    return (advanced, density)


def solution(mesh):
    return jax.shard_map(
        shards,
        mesh=mesh,
        in_specs=(
            P("field", None, "azim", None),
            P("field", "azim", None),
            P("azim", "field"),
            P("azim", "field"),
            P("azim", "field"),
            P(),
            P(),
        ),
        out_specs=(P("field", None, "azim", None), P("azim", "field")),
        check_vma=False,
    )
```

profile of v0, /device:TPU:0, one launch (start us, length us, event | category | flops | bytes accessed | tf_op | source)
XLA Modules:
  0.0 186.6 jit_solution(2838586821642574709)
XLA Ops:
  7.2 0.0 all-reduce.3.cloned.1.call-start
  7.2 6.0 %reduce_sum.27 = f32[10,16,1024]{2,1,0:T(8,128)} reduce(f32[16,10,16,1024]{3,2,1,0:T(8,128)} %param.7, f32[]{:T(128)} %constant.8.clone.1), dimensions={0}, to_apply=%region_0.0 | reduce | flops 2457600 | bytes 11141124 | tf_op jit(solution)/shard_map/reduce_sum | solution.py:62
  13.2 0.0 all-reduce.3.cloned.1.call-update
  13.2 0.0 copy-start.3
  13.2 0.0 copy-start.4
  13.2 0.0 copy-start.5
  13.3 0.0 copy-start.2
  13.3 0.0 copy-start.6
  13.3 0.0 copy-start.7
  13.3 0.0 all-reduce.5.cloned.1.call-start
  13.3 10.5 %copy.19 = f32[16,10,16,1024]{3,0,2,1:T(8,128)S(1)} copy(f32[16,10,16,1024]{3,2,1,0:T(8,128)} %param.7) | data formatting | bytes 20971520 | tf_op args[0]
  23.9 0.0 copy-start
  23.9 1.4 fusion.14
  25.3 4.5 %collective-permute-start = (f32[16,10,1,1024]{3,0,2,1:T(8,128)}, f32[16,10,1,1024]{3,0,2,1:T(8,128)S(1)}, u32[]{:S(2)}, u32[]{:S(2)}) collective-permute-start(f32[16,10,1,1024]{3,0,2,1:T(8,128)} %get-tuple-element.8), channel_id=1, source_target_pairs={{1,0},{2,1},{3,2},{4,3},{5,4},{6,5},{7,6},{0,7},{9,8},{10,9},{11,1... | collective-permute-start | bytes 1966088 | tf_op jit(solution)/shard_map/ppermute | solution.py:21
  29.8 0.0 collective-permute-start.1
  29.8 0.0 copy-done.3
  29.8 8.3 %all_gather.10 = f32[16,1024]{1,0:T(8,128)S(1)} all-gather(f32[16,256]{1,0:T(8,128)S(1)} %copy-done.3), channel_id=1, replica_groups=mesh['field'=4,'azim'=8] {'field'}, dimensions={1}, use_global_device_ids=true | all-gather | bytes 81920 | tf_op jit(solution)/shard_map/all_gather | solution.py:80
  38.1 0.0 copy-done.4
  38.1 8.2 %all_gather.9 = f32[16,1024]{1,0:T(8,128)S(1)} all-gather(f32[16,256]{1,0:T(8,128)S(1)} %copy-done.4), channel_id=1, replica_groups=mesh['field'=4,'azim'=8] {'field'}, dimensions={1}, use_global_device_ids=true | all-gather | bytes 81920 | tf_op jit(solution)/shard_map/all_gather | solution.py:79
  46.4 0.0 copy-done.5
  46.4 7.4 %all_gather.11 = f32[16,1024]{1,0:T(8,128)S(1)} all-gather(f32[16,256]{1,0:T(8,128)S(1)} %copy-done.5), channel_id=1, replica_groups=mesh['field'=4,'azim'=8] {'field'}, dimensions={1}, use_global_device_ids=true | all-gather | bytes 81920 | tf_op jit(solution)/shard_map/all_gather | solution.py:81
  53.8 0.6 copy.18
  54.4 0.6 negate_multiply_fusion
  55.1 0.6 broadcast_multiply_fusion.2
  55.7 0.0 copy-done
  55.7 0.3 fusion.4
  56.0 7.4 %all-reduce.3.cloned.1.call-done = f32[10,16,1024]{2,1,0:T(8,128)} async-done(((f32[10,16,1024]{2,1,0:T(8,128)}), f32[10,16,1024]{2,1,0:T(8,128)}) %all-reduce.3.cloned.1.call-update) | async-done | bytes 655376 | tf_op jit(solution)/shard_map/psum | solution.py:57
  63.3 1.1 broadcast_multiply_fusion.1
  64.5 0.0 collective-permute-done
  64.5 0.0 collective-permute-done.1
  64.5 17.5 %fusion.12 = (f32[10,16,1024]{2,1,0:T(8,128)}, f32[16,10,16,1024]{3,0,2,1:T(8,128)}) fusion(f32[16,16,1024]{2,0,1:T(8,128)S(1)} %copy.18, f32[16,1024]{1,0:T(8,128)S(1)} %sqrt_multiply_fusion, f32[16,10,16,1024]{3,0,2,1:T(8,128)} %copy-done, f32[10]{0:T(128)S(1)} %copy-done.6, f32[16,16,1024]{2,0,1:T(8,128)S(1)} %fusion.4, f32[10]{0:T(128)S(1)} %copy-done.7, ...), kind=kLoop, calls=%fused_computation.28 | loop fusion | flops 57507840 | bytes 25952336 | tf_op jit(solution)/shard_map/reduce_sum | solution.py:62
  82.0 0.0 all-reduce.5.cloned.1.call-update
  82.0 0.0 reduce-scatter.2.cloned.1.call-start
  82.1 1.4 fusion.13
  83.5 0.1 collective-permute-start.3
  83.5 3.5 %collective-permute-start.2 = (f32[16,10,1,1024]{3,0,2,1:T(8,128)S(1)}, f32[16,10,1,1024]{3,0,2,1:T(8,128)}, u32[]{:S(2)}, u32[]{:S(2)}) collective-permute-start(f32[16,10,1,1024]{3,0,2,1:T(8,128)S(1)} %get-tuple-element.7), channel_id=1, source_target_pairs={{1,0},{2,1},{3,2},{4,3},{5,4},{6,5},{7,6},{0,7},{9,8},{10,9},{11,1... | collective-permute-start | bytes 1966088 | tf_op jit(solution)/shard_map/ppermute | solution.py:21
  87.1 1.5 fusion.9
  88.6 40.3 %all-reduce.5.cloned.1.call-done = f32[10,16,1024]{2,1,0:T(8,128)} async-done(((f32[10,16,1024]{2,1,0:T(8,128)}), f32[10,16,1024]{2,1,0:T(8,128)}) %all-reduce.5.cloned.1.call-update) | async-done | bytes 655376 | tf_op jit(solution)/shard_map/psum | solution.py:57
  129.0 1.1 broadcast_multiply_fusion
  130.1 0.0 collective-permute-done.3
  130.1 0.0 collective-permute-done.2
  130.1 19.5 %add_multiply_fusion = f32[16,10,16,1024]{3,0,2,1:T(8,128)S(1)} fusion(f32[16,10,16,1024]{3,0,2,1:T(8,128)} %get-tuple-element.5, f32[16,10,1,1024]{3,0,2,1:T(8,128)} %collective-permute-done.2, f32[16,10,1,1024]{3,0,2,1:T(8,128)} %collective-permute-done.3, f32[16,16,1024]{2,0,1:T(8,128)S(1)} %fusion.9, f32[10,16,1024]{2,1,0:T(8,128)S(1)} %broadcast_multiply_fusion, ...), kind=kLoop, calls=%fused_computation.4 | loop fusion | flops 60293120 | bytes 35782736 | tf_op jit(solution)/shard_map/add | solution.py:85
  149.6 4.0 %copy-done.1 = f32[16,10,16,1024]{3,0,2,1:T(8,128)} copy-done((f32[16,10,16,1024]{3,0,2,1:T(8,128)}, f32[16,10,16,1024]{3,0,2,1:T(8,128)S(1)}, u32[]{:S(2)}) %copy-start.1) | copy-done | bytes 10485784
  153.6 0.9 fusion.11
  154.4 0.0 reduce-scatter.2.cloned.1.call-update
  154.5 14.1 %copy.20 = f32[16,10,16,1024]{3,2,1,0:T(8,128)} copy(f32[16,10,16,1024]{3,0,2,1:T(8,128)} %copy-done.1) | data formatting | bytes 20971520
  168.6 10.1 %reduce-scatter.2.cloned.1.call-done = f32[16,256]{1,0:T(8,128)} async-done(((f32[16,1024]{1,0:T(8,128)}), f32[16,256]{1,0:T(8,128)}) %reduce-scatter.2.cloned.1.call-update) | async-done | bytes 16400 | tf_op jit(solution)/shard_map/reduce_scatter | solution.py:87
  178.7 1.3 multiply_divide_fusion
  (5 shorter events, 0.0 us)
Async XLA Ops:
  7.2 56.2 %all-reduce.3.cloned.1.call-start = ((), (), s32[]{:S(2)}) async-start(), calls=%async_computation.1 | async-start | bytes 1310720 | tf_op jit(solution)/shard_map/psum | solution.py:57
  13.2 16.6 %copy-start.3 = (f32[16,256]{1,0:T(8,128)S(1)}, f32[16,256]{1,0:T(8,128)}, u32[]{:S(2)}) copy-start(f32[16,256]{1,0:T(8,128)} %param.10) | copy-start | bytes 49156
  13.2 24.9 %copy-start.4 = (f32[16,256]{1,0:T(8,128)S(1)}, f32[16,256]{1,0:T(8,128)}, u32[]{:S(2)}) copy-start(f32[16,256]{1,0:T(8,128)} %param.9) | copy-start | bytes 49156
  13.2 33.1 %copy-start.5 = (f32[16,256]{1,0:T(8,128)S(1)}, f32[16,256]{1,0:T(8,128)}, u32[]{:S(2)}) copy-start(f32[16,256]{1,0:T(8,128)} %param.11) | copy-start | bytes 49156
  13.3 40.5 %copy-start.2 = (f32[16,16,1024]{2,1,0:T(8,128)S(1)}, f32[16,16,1024]{2,1,0:T(8,128)}, u32[]{:S(2)}) copy-start(f32[16,16,1024]{2,1,0:T(8,128)} %param.8) | copy-start | bytes 3145732
  13.3 51.2 %copy-start.6 = (f32[10]{0:T(128)S(1)}, f32[10]{0:T(128)}, u32[]{:S(2)}) copy-start(f32[10]{0:T(128)} %param.13) | copy-start | bytes 124
  13.3 51.2 %copy-start.7 = (f32[10]{0:T(128)S(1)}, f32[10]{0:T(128)}, u32[]{:S(2)}) copy-start(f32[10]{0:T(128)} %param.12) | copy-start | bytes 124
  13.3 115.7 %all-reduce.5.cloned.1.call-start = ((), (), s32[]{:S(2)}) async-start(), calls=%async_computation.2 | async-start | bytes 1310720 | tf_op jit(solution)/shard_map/psum | solution.py:57
  23.9 31.8 %copy-start = (f32[16,10,16,1024]{3,0,2,1:T(8,128)}, f32[16,10,16,1024]{3,0,2,1:T(8,128)S(1)}, u32[]{:S(2)}) copy-start(f32[16,10,16,1024]{3,0,2,1:T(8,128)S(1)} %copy.19) | copy-start | bytes 31457284
  25.3 39.2 %collective-permute-start = (f32[16,10,1,1024]{3,0,2,1:T(8,128)}, f32[16,10,1,1024]{3,0,2,1:T(8,128)S(1)}, u32[]{:S(2)}, u32[]{:S(2)}) collective-permute-start(f32[16,10,1,1024]{3,0,2,1:T(8,128)} %get-tuple-element.8), channel_id=1, source_target_pairs={{1,0},{2,1},{3,2},{4,3},{5,4},{6,5},{7,6},{0,7},{9,8},{10,9},{11,1... | collective-permute-start | bytes 1966088 | tf_op jit(solution)/shard_map/ppermute | solution.py:21
  29.8 34.7 %collective-permute-start.1 = (f32[16,10,1,1024]{3,0,2,1:T(8,128)}, f32[16,10,1,1024]{3,0,2,1:T(8,128)S(1)}, u32[]{:S(2)}, u32[]{:S(2)}) collective-permute-start(f32[16,10,1,1024]{3,0,2,1:T(8,128)} %get-tuple-element.9), channel_id=1, source_target_pairs={{0,1},{1,2},{2,3},{3,4},{4,5},{5,6},{6,7},{7,0},{8,9},{9,10},{10,1... | collective-permute-start | bytes 1966088 | tf_op jit(solution)/shard_map/ppermute | solution.py:18
  82.0 96.7 %reduce-scatter.2.cloned.1.call-start = ((), (), s32[]{:S(2)}) async-start(), calls=%async_computation.3 | async-start | bytes 81920 | tf_op jit(solution)/shard_map/reduce_scatter | solution.py:87
  83.5 46.6 %collective-permute-start.3 = (f32[16,10,1,1024]{3,0,2,1:T(8,128)S(1)}, f32[16,10,1,1024]{3,0,2,1:T(8,128)}, u32[]{:S(2)}, u32[]{:S(2)}) collective-permute-start(f32[16,10,1,1024]{3,0,2,1:T(8,128)S(1)} %get-tuple-element.6), channel_id=1, source_target_pairs={{0,1},{1,2},{2,3},{3,4},{4,5},{5,6},{6,7},{7,0},{8,9},{9,10},{10,1... | collective-permute-start | bytes 1966088 | tf_op jit(solution)/shard_map/ppermute | solution.py:18
  83.5 46.6 %collective-permute-start.2 = (f32[16,10,1,1024]{3,0,2,1:T(8,128)S(1)}, f32[16,10,1,1024]{3,0,2,1:T(8,128)}, u32[]{:S(2)}, u32[]{:S(2)}) collective-permute-start(f32[16,10,1,1024]{3,0,2,1:T(8,128)S(1)} %get-tuple-element.7), channel_id=1, source_target_pairs={{1,0},{2,1},{3,2},{4,3},{5,4},{6,5},{7,6},{0,7},{9,8},{10,9},{11,1... | collective-permute-start | bytes 1966088 | tf_op jit(solution)/shard_map/ppermute | solution.py:21
  149.6 4.0 %copy-start.1 = (f32[16,10,16,1024]{3,0,2,1:T(8,128)}, f32[16,10,16,1024]{3,0,2,1:T(8,128)S(1)}, u32[]{:S(2)}) copy-start(f32[16,10,16,1024]{3,0,2,1:T(8,128)S(1)} %add_multiply_fusion) | copy-start | bytes 31457284
Sparse Core Ops, SparseCore 0:
  13.3 49.9 all-reduce.2
  82.2 46.7 all-reduce.4
  154.6 24.0 reduce-scatter.1
where the time goes:
time: 187 us
  waiting for transfers between devices  57.9 us (31%)
  other arithmetic  50.5 us (27%)
  local copies, waits for them, and re-layouts  32 us (17%)
  blocking collectives  24 us (13%)
  between operations  13.9 us (7%)
  starting transfers between devices  8.23 us (4%)
    psum x2, waiting for transfers between devices, field_average(): return lax.psum(local_sum, 'field') / NF  47.7 us
    unnamed x19, local copies, waits for them, and re-layouts  29.3 us
    reduce_sum x2, other arithmetic, rim_segment(): average = field_average(jnp.sum(state, axis=0))  23.5 us
    add x1, other arithmetic, shards(): advanced = 0.5 * scalars + 0.5 * segment_two  19.5 us
    reduce_scatter x1, waiting for transfers between devices, shards(): lax.psum_scatter(jnp.sum(heating, axis=0), 'field', scatter_dimension=1,...  10.1 us
    all_gather x1, blocking collectives, shards(): lax.all_gather(diffusivity, 'field', axis=1, tiled=True)  8.32 us
    all_gather x1, blocking collectives, shards(): lax.all_gather(velocity, 'field', axis=1, tiled=True)  8.22 us
    ppermute x2, starting transfers between devices, with_halo(): lax.ppermute(lax.slice_in_dim(block, 0, width, axis=dim), axis, backward)  8.05 us
  transfers between devices with their start and end apart: 7, of which 3 were waited for; matrix products, arithmetic and copies ran while one was open for 18% of the time, Pallas kernels for 0%

commit v1 on v0

v1 whole, which is shorter than its diff:
```python
import functools

import jax
import jax.numpy as jnp
from jax import lax
from jax.experimental import pallas as pl
from jax.experimental.pallas import tpu as pltpu
from jax.sharding import PartitionSpec as P

step_size = 0.2
LANES = 128
SUB = 8
F32 = jnp.float32


def ring(count, shift):
    return [(i, (i + shift) % count) for i in range(count)]


def phases(fields):
    return fields.bit_length() - 1


def swap_pairs(fields, slabs, phase):
    bits = phases(fields)
    pairs = []
    for field in range(fields):
        for slab in range(slabs):
            partner = field ^ (1 << ((phase + slab % 2) % bits))
            pairs.append((field * slabs + slab, partner * slabs + slab))
    return pairs


def swap(value, fields, slabs, phase):
    return lax.ppermute(value, ("field", "azim"), swap_pairs(fields, slabs, phase))


def split_rows(value):
    return [value[i : i + SUB] for i in range(0, value.shape[0], SUB)]


def row_index(shape):
    return lax.broadcasted_iota(jnp.int32, shape, 0)


def ups(parts, last, edge):
    turned = [pltpu.roll(part, SUB - 1, 0) for part in parts]
    after = turned[1:] + [edge]
    return [
        turned[i] if after[i] is None else jnp.where(last, after[i], turned[i])
        for i in range(len(parts))
    ]


def downs(parts, first, edge):
    turned = [pltpu.roll(part, 1, 0) for part in parts]
    before = [edge] + turned[:-1]
    return [
        turned[i] if before[i] is None else jnp.where(first, before[i], turned[i])
        for i in range(len(parts))
    ]


def burn(scalar):
    heating = 1.0 + 0.5 * scalar * scalar
    return jnp.exp(1.0 - 1.0 / heating)


def sums_kernel(q_ref, w_ref, sum_ref, noise_ref, mass_ref, burn_ref, lo_ref, lo1_ref, hi_ref, hi1_ref, b_scr):
    F, S, R, width = q_ref.shape
    tiles = R // SUB
    group = S // 2 if S % 2 == 0 else S
    row = row_index((SUB, LANES))
    first, last = row == 0, row == SUB - 1
    zero = jnp.zeros((SUB, LANES), F32)
    for lane in range(0, width, LANES):
        cells = pl.ds(lane, LANES)

        def burning(f, total):
            b = [burn(x) for x in split_rows(q_ref[f, 0, :, cells])]
            for i in range(tiles):
                b_scr[f, pl.ds(i * SUB, SUB), :] = b[i]
            return tuple(t + x for t, x in zip(total, b))

        total = lax.fori_loop(0, F, burning, (zero,) * tiles, unroll=4)
        for i in range(tiles):
            burn_ref[pl.ds(i * SUB, SUB), cells] = total[i]

        for start in range(0, S, group):

            def body(f, carry):
                w = split_rows(w_ref[f, :, cells])
                b = split_rows(b_scr[f])
                out = []
                for g in range(group):
                    q = split_rows(q_ref[f, start + g, :, cells])
                    up, down = ups(q, last, zero), downs(q, first, zero)
                    for i in range(tiles):
                        a, n, m = carry[g * tiles + i]
                        out.append((a + q[i], n + w[i] * (up[i] - down[i]), m + b[i] * q[i]))
                return tuple(out)

            sums = lax.fori_loop(0, F, body, ((zero, zero, zero),) * (group * tiles), unroll=2)
            for g in range(group):
                for i in range(tiles):
                    at = (start + g, pl.ds(i * SUB, SUB), cells)
                    sum_ref[at], noise_ref[at], mass_ref[at] = sums[g * tiles + i]
    for s in range(S):
        rows = pl.ds(s * F, F)
        lo_ref[rows, :] = q_ref[:, s, 0, :]
        lo1_ref[rows, :] = q_ref[:, s, 1, :]
        hi_ref[rows, :] = q_ref[:, s, R - 1, :]
        hi1_ref[rows, :] = q_ref[:, s, R - 2, :]


def field_sums(q, w, width):
    F, S, R, N = q.shape
    cube = jax.ShapeDtypeStruct((S, R, N), F32)
    rows = jax.ShapeDtypeStruct((S * F, N), F32)
    cube_spec = pl.BlockSpec((S, R, width), lambda c: (0, 0, c))
    rows_spec = pl.BlockSpec((S * F, width), lambda c: (0, c))
    return pl.pallas_call(
        sums_kernel,
        grid=(N // width,),
        in_specs=[
            pl.BlockSpec((F, S, R, width), lambda c: (0, 0, 0, c)),
            pl.BlockSpec((F, R, width), lambda c: (0, 0, c)),
        ],
        out_specs=[cube_spec] * 3 + [pl.BlockSpec((R, width), lambda c: (0, c))] + [rows_spec] * 4,
        out_shape=[cube] * 3 + [jax.ShapeDtypeStruct((R, N), F32)] + [rows] * 4,
        scratch_shapes=[pltpu.VMEM((F, R, LANES), F32)],
        compiler_params=pltpu.CompilerParams(vmem_limit_bytes=24 << 20),
        name="sums",
    )(q, w)


def rim_kernel(
    order_ref, rate_ref, goal_ref, gas_ref, sum_ref, noise_ref, mass_ref, burn_ref, lo_ref, lo1_ref,
    hi_ref, hi1_ref, below_ref, above_ref, w_ref,
    total_ref, send_lo_ref, send_hi_ref, coef_ref, edge_ref,
):
    del order_ref
    S, R, width = sum_ref.shape
    F = w_ref.shape[0]
    velocity, diffusivity, mix_rate = gas_ref[0, 0], gas_ref[0, 1], gas_ref[0, 2]
    half = 0.5 * jnp.sqrt(2.0 * diffusivity)
    up_coef = step_size * diffusivity - (0.5 * step_size) * velocity
    down_coef = step_size * diffusivity + (0.5 * step_size) * velocity
    keep = 1.0 - (2.0 * step_size) * diffusivity
    mix = (0.5 * step_size) * mix_rate
    own = keep - mix
    coef_ref[0] = up_coef
    coef_ref[1] = down_coef
    coef_ref[2] = own
    coef_ref[3] = half
    coef_ref[4] = mix
    first_row, last_row = pl.ds(0, 1), pl.ds(R - 1, 1)
    w_lo, w_hi = w_ref[:, 0, :], w_ref[:, R - 1, :]

    def at(value, r):
        return value[r : r + 1]

    lo_up = at(up_coef, 0) + at(half, 0) * w_lo
    lo_down = at(down_coef, 0) - at(half, 0) * w_lo
    hi_up = at(up_coef, R - 1) + at(half, R - 1) * w_hi
    hi_down = at(down_coef, R - 1) - at(half, R - 1) * w_hi
    edge_ref[0] = 0.5 * lo_down
    edge_ref[1] = 0.5 * hi_up
    lo_burn = step_size * burn(lo_ref[pl.ds(0, F), :])
    hi_burn = step_size * burn(hi_ref[pl.ds(0, F), :])
    row = row_index((R, width))
    first, last = row == 0, row == R - 1
    burned = burn_ref[...]
    for s in range(S):
        rows = pl.ds(s * F, F)
        rate, goal = rate_ref[s], goal_ref[s]
        below, above = below_ref[rows, :], above_ref[rows, :]
        q_lo, q_hi = lo_ref[rows, :], hi_ref[rows, :]
        send_lo_ref[rows, :] = (
            at(own, 0) * q_lo
            + lo_up * lo1_ref[rows, :]
            + lo_down * below
            + (rate * lo_burn) * (goal - q_lo)
        )
        send_hi_ref[rows, :] = (
            at(own, R - 1) * q_hi
            + hi_up * above
            + hi_down * hi1_ref[rows, :]
            + (rate * hi_burn) * (goal - q_hi)
        )
        sum_below = jnp.sum(below, axis=0, keepdims=True)
        sum_above = jnp.sum(above, axis=0, keepdims=True)
        noise_below = jnp.sum(w_lo * below, axis=0, keepdims=True)
        noise_above = jnp.sum(w_hi * above, axis=0, keepdims=True)
        total_ref[pl.ds(S * R + s, 1), :] = sum_below
        total_ref[pl.ds(S * R + S + s, 1), :] = sum_above
        middle = sum_ref[s]
        upper = jnp.where(last, sum_above, pltpu.roll(middle, R - 1, 0))
        lower = jnp.where(first, sum_below, pltpu.roll(middle, 1, 0))
        noise = noise_ref[s] + jnp.where(last, noise_above, 0.0) - jnp.where(first, noise_below, 0.0)
        total_ref[pl.ds(s * R, R), :] = (
            keep * middle
            + up_coef * upper
            + down_coef * lower
            + half * noise
            + (step_size * rate) * (goal * burned - mass_ref[s])
        )
    send_lo_ref[pl.ds(S * F, SUB), :] = jnp.broadcast_to(at(mix, 0), (SUB, width))
    send_hi_ref[pl.ds(S * F, SUB), :] = jnp.broadcast_to(at(mix, R - 1), (SUB, width))
    tail = total_ref.shape[0] - (S * R + 2 * S)
    if tail:
        total_ref[pl.ds(S * R + 2 * S, tail), :] = jnp.zeros((tail, width), F32)


def rim(order, rate, goal, gas, sums, packed, below, above, w):
    total, noise, mass, burned = sums
    S, R, N = total.shape
    F = w.shape[0]
    width = gas.shape[-1]
    height = -(-(S * R + 2 * S) // SUB) * SUB
    cube_spec = pl.BlockSpec((S, R, width), lambda c, o: (0, 0, c))
    rows_spec = pl.BlockSpec((S * F, width), lambda c, o: (0, c))
    send_spec = pl.BlockSpec((S * F + SUB, width), lambda c, o: (0, c))
    smem = pl.BlockSpec(memory_space=pltpu.SMEM)
    return pl.pallas_call(
        rim_kernel,
        grid_spec=pltpu.PrefetchScalarGridSpec(
            num_scalar_prefetch=1,
            grid=(N // width,),
            in_specs=[smem, smem, pl.BlockSpec((1, 3, R, width), lambda c, o: (o[c], 0, 0, 0))]
            + [cube_spec] * 3
            + [pl.BlockSpec((R, width), lambda c, o: (0, c))]
            + [rows_spec] * 6
            + [pl.BlockSpec((F, R, width), lambda c, o: (0, 0, c))],
            out_specs=[
                pl.BlockSpec((height, width), lambda c, o: (0, c)),
                send_spec,
                send_spec,
                pl.BlockSpec((5, R, width), lambda c, o: (0, 0, c)),
                pl.BlockSpec((2, F, width), lambda c, o: (0, 0, c)),
            ],
        ),
        out_shape=[
            jax.ShapeDtypeStruct((height, N), F32),
            jax.ShapeDtypeStruct((S * F + SUB, N), F32),
            jax.ShapeDtypeStruct((S * F + SUB, N), F32),
            jax.ShapeDtypeStruct((5, R, N), F32),
            jax.ShapeDtypeStruct((2, F, N), F32),
        ],
        compiler_params=pltpu.CompilerParams(vmem_limit_bytes=24 << 20),
        name="rim",
    )(order, rate, goal, gas, total, noise, mass, burned, *packed, below, above, w)


def segments_kernel(
    count, rate_ref, goal_ref, q_ref, w_ref, coef_ref, sum_ref, got_ref, below_ref, above_ref, out_ref,
    pull_scr, edge_scr,
):
    F, S, R, width = q_ref.shape
    tiles = R // SUB
    row = row_index((SUB, LANES))
    first, last = row == 0, row == SUB - 1
    for s in range(S):
        pull_scr[s] = (coef_ref[4] * (1.0 / count)) * (sum_ref[s] + got_ref[s])
    for lane in range(width // LANES):
        for i, ref in enumerate((below_ref, above_ref)):
            edge_scr[i, lane] = ref[:, pl.ds(lane * LANES, LANES)]

    def tile(step, carry):
        lane, f = step // F, step % F
        cells = pl.ds(pl.multiple_of(lane * LANES, LANES), LANES)
        up_coef, down_coef, own, half = (split_rows(coef_ref[i, :, cells]) for i in range(4))
        w = split_rows(w_ref[f, :, cells])
        kick = [h * x for h, x in zip(half, w)]
        rise = [c + k for c, k in zip(up_coef, kick)]
        fall = [c - k for c, k in zip(down_coef, kick)]
        rise_in = rise[:-1] + [jnp.where(last, 0.0, rise[-1])]
        fall_in = [jnp.where(first, 0.0, fall[0])] + fall[1:]
        hot = None
        hot_next = None
        for s in range(S):
            rate, goal = step_size * rate_ref[s], goal_ref[s]
            q = split_rows(q_ref[f, s, :, cells])
            pull = split_rows(pull_scr[s, :, cells])
            below, above = (
                jnp.broadcast_to(edge_scr[i, lane, pl.ds(s * F + f, 1), :], (SUB, LANES)) for i in range(2)
            )
            up, down = ups(q, last, above), downs(q, first, below)
            if s == 0:
                hot = [burn(x) for x in q]
            one = [
                own[i] * q[i] + rise[i] * up[i] + fall[i] * down[i] + pull[i] + (rate * hot[i]) * (goal - q[i])
                for i in range(tiles)
            ]
            if s == 0:
                hot_next = [burn(x) for x in one]
            up, down = ups(one, last, None), downs(one, first, None)
            for i in range(tiles):
                two = (
                    own[i] * one[i]
                    + rise_in[i] * up[i]
                    + fall_in[i] * down[i]
                    + (rate * hot_next[i]) * (goal - one[i])
                )
                out_ref[f, s, pl.ds(i * SUB, SUB), cells] = 0.5 * (q[i] + two)
        return carry

    lax.fori_loop(0, F * (width // LANES), tile, 0)


def segments(count, rate, goal, q, w, coef, total, got, below, above, width):
    F, S, R, N = q.shape
    big = pl.BlockSpec((F, S, R, width), lambda c: (0, 0, 0, c))
    cube_spec = pl.BlockSpec((S, R, width), lambda c: (0, 0, c))
    rows_spec = pl.BlockSpec((S * F, width), lambda c: (0, c))
    smem = pl.BlockSpec(memory_space=pltpu.SMEM)
    return pl.pallas_call(
        functools.partial(segments_kernel, count),
        grid=(N // width,),
        in_specs=[
            smem,
            smem,
            big,
            pl.BlockSpec((F, R, width), lambda c: (0, 0, c)),
            pl.BlockSpec((5, R, width), lambda c: (0, 0, c)),
            cube_spec,
            cube_spec,
            rows_spec,
            rows_spec,
        ],
        out_specs=big,
        out_shape=jax.ShapeDtypeStruct((F, S, R, N), F32),
        scratch_shapes=[
            pltpu.VMEM((S, R, width), F32),
            pltpu.VMEM((2, width // LANES, S * F, LANES), F32),
        ],
        compiler_params=pltpu.CompilerParams(vmem_limit_bytes=24 << 20),
        name="segments",
    )(rate, goal, q, w, coef, total, got, below, above)


def edge_rows(count, scalars, R, total_ref, got_ref, edge_ref, sides, add_scr):
    F, N = edge_ref.shape[1:]
    S = (sides[0].shape[0] - SUB) // F
    for i, ref in enumerate(sides):
        mix = ref[pl.ds(S * F, 1), :] * (1.0 / count)
        for j, s in enumerate(scalars):
            at = pl.ds(S * R + i * S + s, 1)
            value = edge_ref[i] * (ref[pl.ds(s * F, F), :] + mix * (total_ref[at, :] + got_ref[at, :]))
            for lane in range(N // LANES):
                add_scr[i, j, lane] = value[:, lane * LANES : (lane + 1) * LANES]


def finish_scalar(count, s, j, c_ref, total_ref, got_ref, coef_ref, out_ref, add_scr, heat_ref=None):
    F, _, R, N = c_ref.shape
    row = row_index((SUB, LANES))
    first, last = row == 0, row == SUB - 1
    rows = pl.ds(pl.multiple_of(s * R, R), R)
    for lane in range(N // LANES):
        cells = pl.ds(lane * LANES, LANES)
        pull = split_rows(coef_ref[4, :, cells] * (0.5 / count) * (total_ref[rows, cells] + got_ref[rows, cells]))

        def body(f, heat):
            add_lo, add_hi = (
                jnp.broadcast_to(add_scr[i, j, lane, pl.ds(f, 1), :], (SUB, LANES)) for i in range(2)
            )
            value = [x + p for x, p in zip(split_rows(c_ref[f, 0, :, cells]), pull)]
            value[0] = value[0] + jnp.where(first, add_lo, 0.0)
            value[-1] = value[-1] + jnp.where(last, add_hi, 0.0)
            for i, x in enumerate(value):
                out_ref[f, 0, pl.ds(i * SUB, SUB), cells] = x
            return tuple(h + 0.5 * x * x for h, x in zip(heat, value)) if heat else heat

        start = () if heat_ref is None else (jnp.full((SUB, LANES), float(F), F32),) * len(pull)
        heat = lax.fori_loop(0, F, body, start, unroll=4)
        for i, h in enumerate(heat):
            heat_ref[pl.ds(i * SUB, SUB), cells] = h


def head_kernel(count, c_ref, total_ref, got_ref, coef_ref, edge_ref, lo_ref, hi_ref, out_ref, heat_ref, add_scr):
    edge_rows(count, [0], c_ref.shape[2], total_ref, got_ref, edge_ref, (lo_ref, hi_ref), add_scr)
    finish_scalar(count, 0, 0, c_ref, total_ref, got_ref, coef_ref, out_ref, add_scr, heat_ref)


def rest_kernel(count, first_out_ref, c_ref, total_ref, got_ref, coef_ref, edge_ref, lo_ref, hi_ref, out_ref, add_scr):
    del first_out_ref
    step = pl.program_id(0)

    @pl.when(step == 0)
    def _():
        scalars = range(1, 1 + add_scr.shape[1])
        edge_rows(count, scalars, c_ref.shape[2], total_ref, got_ref, edge_ref, (lo_ref, hi_ref), add_scr)

    finish_scalar(count, step + 1, step, c_ref, total_ref, got_ref, coef_ref, out_ref, add_scr)


def finish(count, c, total, got, coef, edge, lo, hi):
    F, S, R, N = c.shape

    def whole(value):
        return pl.BlockSpec(value.shape, lambda *_: (0,) * value.ndim)

    small = (total, got, coef, edge, lo, hi)
    params = pltpu.CompilerParams(vmem_limit_bytes=24 << 20)

    def scratch(scalars):
        return [pltpu.VMEM((2, scalars, N // LANES, F, LANES), F32)]

    out_shape = jax.ShapeDtypeStruct((F, S, R, N), F32)
    at_zero = pl.BlockSpec((F, 1, R, N), lambda g: (0, 0, 0, 0))
    at_next = pl.BlockSpec((F, 1, R, N), lambda g: (0, g + 1, 0, 0))
    partial, heat = pl.pallas_call(
        functools.partial(head_kernel, count),
        grid=(1,),
        in_specs=[at_zero] + [whole(x) for x in small],
        out_specs=[at_zero, pl.BlockSpec((R, N), lambda g: (0, 0))],
        out_shape=[out_shape, jax.ShapeDtypeStruct((R, N), F32)],
        scratch_shapes=scratch(1),
        compiler_params=params,
        name="head",
    )(c, *small)
    advanced = pl.pallas_call(
        functools.partial(rest_kernel, count),
        grid=(S - 1,),
        in_specs=[pl.BlockSpec(memory_space=pl.ANY), at_next] + [whole(x) for x in small],
        out_specs=at_next,
        out_shape=out_shape,
        scratch_shapes=scratch(S - 1),
        input_output_aliases={0: 0},
        compiler_params=params,
        name="rest",
    )(partial, c, *small)
    return advanced, heat


def shards(fields, slabs, scalars, wiener, velocity, diffusivity, mix_rate, reaction_rate, equilibrium):
    bits = phases(fields)
    F, S, R, N = scalars.shape
    count = float(F * fields)
    me, slab = lax.axis_index("field"), lax.axis_index("azim")

    gas = jnp.stack([velocity, diffusivity, mix_rate])[None]
    order = jnp.zeros((fields,), jnp.int32)
    away = jnp.arange(fields, dtype=jnp.int32) ^ me
    for phase in range(bits):
        gas = jnp.concatenate([gas, swap(gas, fields, slabs, phase)])
        bit = (phase + slab % 2) % bits
        order = order | (((away >> bit) & 1) << phase)

    *sums, lo, lo1, hi, hi1 = field_sums(scalars, wiener, 2 * LANES)
    below = lax.ppermute(hi, "azim", ring(slabs, 1))
    above = lax.ppermute(lo, "azim", ring(slabs, -1))

    total, got = sums[0], None
    for phase in range(bits):
        total = total if got is None else total + got
        got = swap(total, fields, slabs, phase)

    later, send_lo, send_hi, coef, edge = rim(
        order, reaction_rate, equilibrium, gas, sums, (lo, lo1, hi, hi1), below, above, wiener
    )
    next_lo = lax.ppermute(send_hi, "azim", ring(slabs, 1))
    next_hi = lax.ppermute(send_lo, "azim", ring(slabs, -1))

    later_got = None
    for phase in range(bits):
        later = later if later_got is None else later + later_got
        later_got = swap(later, fields, slabs, phase)

    c = segments(
        count, reaction_rate, equilibrium, scalars, wiener, coef, total, got, below, above, 2 * LANES
    )
    advanced, heat = finish(count, c, later, later_got, coef, edge, next_lo, next_hi)
    for phase in range(bits):
        heat = heat + swap(heat, fields, slabs, phase)
    mine = lax.dynamic_slice_in_dim(heat, me * (N // fields), N // fields, axis=1)
    return advanced, 1.0 / (mine / count)


def solution(mesh):
    return jax.shard_map(
        functools.partial(shards, mesh.shape["field"], mesh.shape["azim"]),
        mesh=mesh,
        in_specs=(
            P("field", None, "azim", None),
            P("field", "azim", None),
            P("azim", "field"),
            P("azim", "field"),
            P("azim", "field"),
            P(),
            P(),
        ),
        out_specs=(P("field", None, "azim", None), P("azim", "field")),
        check_vma=False,
    )
```

time: 187 us -> 125 us (0.67)
  other arithmetic: 50.5 us -> 1.94 us
  Pallas kernels: 0 us -> 35.6 us
  blocking collectives: 24 us -> 0 us
  waiting for transfers between devices: 57.9 us -> 34.6 us
  starting transfers between devices: 8.23 us -> 23 us
  between operations: 13.9 us -> 0.81 us
  local copies, waits for them, and re-layouts: 32 us -> 27.9 us
    psum x2 -> x0, waiting for transfers between devices: 47.7 us -> none  [field_average(): return lax.psum(local_sum, 'field') / NF]
    pallas_call x0 -> x5, Pallas kernels: none -> 35.6 us  [the longest x1 15.4 us: segments(): pl.pallas_call(functools.partial(segments_kernel, count), grid=(N // widt...]
    ppermute x4 -> x12, waiting for transfers between devices: 0.01 us -> 34.6 us  [the longest x8 30.4 us: swap(): lax.ppermute(value, ('field', 'azim'), swap_pairs(fields, slabs, phase))]
    reduce_sum x3 -> x0, other arithmetic: 24.4 us -> none  [the longest x2 23.5 us: rim_segment(): average = field_average(jnp.sum(state, axis=0))]
    all_gather x3 -> x0, blocking collectives: 24 us -> none  [the longest x1 8.32 us: shards(): lax.all_gather(diffusivity, 'field', axis=1, tiled=True)]
    add x1 -> x3, other arithmetic: 19.5 us -> 1.29 us  [the longest x1 1.18 us: shards(): total = total if got is None else total + got]
    ppermute x4 -> x12, starting transfers between devices: 8.11 us -> 23 us  [the longest x8 14.9 us: swap(): lax.ppermute(value, ('field', 'azim'), swap_pairs(fields, slabs, phase))]
    reduce_scatter x1 -> x0, waiting for transfers between devices: 10.1 us -> none  [shards(): lax.psum_scatter(jnp.sum(heating, axis=0), 'field', scatter_dimension=1,...]
  transfers between devices with their start and end apart: 7 -> 12, of which waited for: 3 -> 8; matrix products, arithmetic and copies ran while one was open for 18% -> 1% of each run, Pallas kernels for 0% -> 18%
where the time goes in v1:
time: 125 us; the launch traced here: 124 us
  Pallas kernels  35.6 us (28%)
  waiting for transfers between devices  34.6 us (28%)
  local copies, waits for them, and re-layouts  27.9 us (22%)
  starting transfers between devices  23 us (18%)
  other arithmetic  1.94 us (2%)
    ppermute x8, waiting for transfers between devices, swap(): lax.ppermute(value, ('field', 'azim'), swap_pairs(fields, slabs, phase))  30.4 us
    unnamed x62, local copies, waits for them, and re-layouts  27.9 us
    pallas_call x1, Pallas kernels, segments(): pl.pallas_call(functools.partial(segments_kernel, count), grid=(N // widt...  15.4 us
    ppermute x8, starting transfers between devices, swap(): lax.ppermute(value, ('field', 'azim'), swap_pairs(fields, slabs, phase))  14.9 us
    pallas_call x1, Pallas kernels, field_sums(): pl.pallas_call(sums_kernel, grid=(N // width,), in_specs=[pl.BlockSpec((F...  7.95 us
    pallas_call x1, Pallas kernels, finish(): pl.pallas_call(functools.partial(rest_kernel, count), grid=(S - 1,), in_s...  6.77 us
    ppermute x1, starting transfers between devices, shards(): above = lax.ppermute(lo, 'azim', ring(slabs, -1))  4.03 us
    pallas_call x1, Pallas kernels, rim(): pl.pallas_call(rim_kernel, grid_spec=pltpu.PrefetchScalarGridSpec(num_sca...  4.01 us
  transfers between devices with their start and end apart: 12, of which 8 were waited for; matrix products, arithmetic and copies ran while one was open for 1% of the time, Pallas kernels for 18%

profile of v1, /device:TPU:0, one launch (start us, length us, event | category | flops | bytes accessed | tf_op | source)
XLA Modules:
  0.0 123.8 jit_solution(12303669456050948477)
XLA Ops:
  0.6 0.0 copy-start.2
  0.6 4.0 %copy-done.2 = f32[16,10,16,1024]{3,2,1,0:T(8,128)S(1)} copy-done((f32[16,10,16,1024]{3,2,1,0:T(8,128)S(1)}, f32[16,10,16,1024]{3,2,1,0:T(8,128)}, u32[]{:S(2)}) %copy-start.2) | copy-done | bytes 10485784
  4.6 1.2 copy-done.4
  5.9 8.0 %sums.1 = (f32[10,16,1024]{2,1,0:T(8,128)}, f32[10,16,1024]{2,1,0:T(8,128)S(1)}, f32[10,16,1024]{2,1,0:T(8,128)S(1)}, f32[16,1024]{1,0:T(8,128)S(1)}, f32[160,10...) custom-call(f32[16,10,16,1024]{3,2,1,0:T(8,128)S(1)} %copy-done.2, ...), custom_call_target="tpu_custom_call" | custom-call | tf_op jit(solution)/shard_map/sums/pallas_call | solution.py:122
  13.8 0.8 copy-done.12
  14.7 0.8 copy-done.14
  15.5 0.8 copy-done.18
  16.3 0.8 copy-done.20
  17.2 0.6 copy-done.24
  17.8 0.5 collective-permute-start.2
  18.3 4.0 %collective-permute-start.3 = (f32[160,1024]{1,0:T(8,128)S(1)}, f32[160,1024]{1,0:T(8,128)S(1)}, u32[]{:S(2)}, u32[]{:S(2)}) collective-permute-start(f32[160,1024]{1,0:T(8,128)S(1)} %get-tuple-element.21.lo_ref), channel_id=1, source_target_pairs={{0,7},{1,0},{2,1},{3,2},{4,3},{5,4},{6,5},{7,6},{8,15},{9,8},{10,9... | collective-permute-start | bytes 1966088 | tf_op jit(solution)/shard_map/ppermute | solution.py:452
  22.3 2.1 %collective-permute-start = (f32[1,3,16,256]{3,2,1,0:T(8,128)S(1)}, f32[1,3,16,256]{3,2,1,0:T(8,128)S(1)}, u32[]{:S(2)}, u32[]{:S(2)}) collective-permute-start(f32[1,3,16,256]{3,2,1,0:T(8,128)S(1)} %maximum_bitcast_fusion), channel_id=1, source_target_pairs={{0,8},{1,17},{2,10},{3,19},{4,12},{5,21},{6,14},{7,23},{8,0},{9,25... | collective-permute-start | bytes 147464 | tf_op jit(solution)/shard_map/ppermute | solution.py:35
  24.4 2.1 %collective-permute-done = f32[1,3,16,256]{3,2,1,0:T(8,128)S(1)} collective-permute-done((f32[1,3,16,256]{3,2,1,0:T(8,128)S(1)}, f32[1,3,16,256]{3,2,1,0:T(8,128)S(1)}, u32[]{:S(2)}, u32[]{:S(2)}) %collective-permute-start) | collective-permute-done | bytes 49184 | tf_op jit(solution)/shard_map/ppermute | solution.py:35
  26.5 2.4 %collective-permute-start.1 = (f32[2,3,16,256]{3,2,1,0:T(8,128)S(1)}, f32[2,3,16,256]{3,2,1,0:T(8,128)S(1)}, u32[]{:S(2)}, u32[]{:S(2)}) collective-permute-start(f32[2,3,16,256]{3,2,1,0:T(8,128)S(1)} %pad_maximum_fusion.1), channel_id=1, source_target_pairs={{0,16},{1,9},{2,18},{3,11},{4,20},{5,13},{6,22},{7,15},{8,24},{9,1... | collective-permute-start | bytes 294920 | tf_op jit(solution)/shard_map/ppermute | solution.py:35
  28.9 2.6 %collective-permute-done.1 = f32[2,3,16,256]{3,2,1,0:T(8,128)S(1)} collective-permute-done((f32[2,3,16,256]{3,2,1,0:T(8,128)S(1)}, f32[2,3,16,256]{3,2,1,0:T(8,128)S(1)}, u32[]{:S(2)}, u32[]{:S(2)}) %collective-permute-start.1) | collective-permute-done | bytes 98336 | tf_op jit(solution)/shard_map/ppermute | solution.py:35
  31.5 3.9 %collective-permute-done.2.below_ref = f32[160,1024]{1,0:T(8,128)S(1)} collective-permute-done((f32[160,1024]{1,0:T(8,128)}, f32[160,1024]{1,0:T(8,128)S(1)}, u32[]{:S(2)}, u32[]{:S(2)}) %collective-permute-start.2) | collective-permute-done | bytes 655392 | tf_op jit(solution)/shard_map/ppermute | solution.py:451
  35.4 0.2 collective-permute-done.3.above_ref
  35.7 1.3 %copy-done.13 = f32[10,16,1024]{2,1,0:T(8,128)S(1)} copy-done((f32[10,16,1024]{2,1,0:T(8,128)S(1)}, f32[10,16,1024]{2,1,0:T(8,128)}, u32[]{:S(2)}) %copy-start.13) | copy-done | bytes 655384
  37.0 1.1 copy-done.15
  38.1 1.1 copy-done.17
  39.2 1.1 copy-done.19
  40.3 1.1 copy-done.21
  41.4 0.8 copy-done.25
  42.2 4.0 %rim.1 = (f32[184,1024]{1,0:T(8,128)S(1)}, f32[168,1024]{1,0:T(8,128)S(1)}, f32[168,1024]{1,0:T(8,128)S(1)}, f32[5,16,1024]{2,1,0:T(8,128)S(1)}, f32[2,16,1024]{2,1,0:T(8,128)S(1)}) custom-call(s32[4]{0:T(128)S(1)} %shift-left_or_fusion.order_ref, f32[10]{0:T(128)S(1)} %copy-done.26, f32[10]{0:T(128)S(1)} %copy-done.27, ...), custom_call_target="tpu_custom_call" | custom-call | tf_op jit(solution)/shard_map/rim/pallas_call | solution.py:225
  46.2 2.3 %collective-permute-start.6 = (f32[184,1024]{1,0:T(8,128)S(1)}, f32[184,1024]{1,0:T(8,128)S(1)}, u32[]{:S(2)}, u32[]{:S(2)}) collective-permute-start(f32[184,1024]{1,0:T(8,128)S(1)} %get-tuple-element.26), channel_id=1, source_target_pairs={{0,8},{1,17},{2,10},{3,19},{4,12},{5,21},{6,14},{7,23},{8,0},{9,25... | collective-permute-start | bytes 2261000 | tf_op jit(solution)/shard_map/ppermute | solution.py:35
  48.6 0.1 collective-permute-start.4
  48.6 9.5 %collective-permute-done.6 = f32[184,1024]{1,0:T(8,128)S(1)} collective-permute-done((f32[184,1024]{1,0:T(8,128)S(1)}, f32[184,1024]{1,0:T(8,128)S(1)}, u32[]{:S(2)}, u32[]{:S(2)}) %collective-permute-start.6) | collective-permute-done | bytes 753696 | tf_op jit(solution)/shard_map/ppermute | solution.py:35
  58.2 0.1 add.34.total_ref
  58.3 2.1 %collective-permute-start.7 = (f32[184,1024]{1,0:T(8,128)S(1)}, f32[184,1024]{1,0:T(8,128)S(1)}, u32[]{:S(2)}, u32[]{:S(2)}) collective-permute-start(f32[184,1024]{1,0:T(8,128)S(1)} %add.34.total_ref), channel_id=1, source_target_pairs={{0,16},{1,9},{2,18},{3,11},{4,20},{5,13},{6,22},{7,15},{8,24},{9,1... | collective-permute-start | bytes 2261000 | tf_op jit(solution)/shard_map/ppermute | solution.py:35
  60.4 0.4 collective-permute-start.8
  60.8 3.1 %collective-permute-start.9 = (f32[168,1024]{1,0:T(8,128)S(1)}, f32[168,1024]{1,0:T(8,128)S(1)}, u32[]{:S(2)}, u32[]{:S(2)}) collective-permute-start(f32[168,1024]{1,0:T(8,128)S(1)} %get-tuple-element.29), channel_id=1, source_target_pairs={{0,7},{1,0},{2,1},{3,2},{4,3},{5,4},{6,5},{7,6},{8,15},{9,8},{10,9... | collective-permute-start | bytes 2064392 | tf_op jit(solution)/shard_map/ppermute | solution.py:463
  63.9 4.5 %collective-permute-done.4 = f32[10,16,1024]{2,1,0:T(8,128)S(1)} collective-permute-done((f32[10,16,1024]{2,1,0:T(8,128)}, f32[10,16,1024]{2,1,0:T(8,128)S(1)}, u32[]{:S(2)}, u32[]{:S(2)}) %collective-permute-start.4) | collective-permute-done | bytes 655392 | tf_op jit(solution)/shard_map/ppermute | solution.py:35
  68.4 1.2 add.33.sum_ref
  69.6 2.4 %collective-permute-start.5 = (f32[10,16,1024]{2,1,0:T(8,128)S(1)}, f32[10,16,1024]{2,1,0:T(8,128)S(1)}, u32[]{:S(2)}, u32[]{:S(2)}) collective-permute-start(f32[10,16,1024]{2,1,0:T(8,128)S(1)} %add.33.sum_ref), channel_id=1, source_target_pairs={{0,16},{1,9},{2,18},{3,11},{4,20},{5,13},{6,22},{7,15},{8,24},{9,1... | collective-permute-start | bytes 1966088 | tf_op jit(solution)/shard_map/ppermute | solution.py:35
  72.0 9.2 %collective-permute-done.5.got_ref = f32[10,16,1024]{2,1,0:T(8,128)S(1)} collective-permute-done((f32[10,16,1024]{2,1,0:T(8,128)S(1)}, f32[10,16,1024]{2,1,0:T(8,128)S(1)}, u32[]{:S(2)}, u32[]{:S(2)}) %collective-permute-start.5) | collective-permute-done | bytes 655392 | tf_op jit(solution)/shard_map/ppermute | solution.py:35
  81.2 1.1 copy-done.11
  82.3 15.4 %segments.1.c_ref = f32[16,10,16,1024]{3,2,1,0:T(8,128)S(1)} custom-call(f32[10]{0:T(128)S(1)} %copy-done.26, f32[10]{0:T(128)S(1)} %copy-done.27, f32[16,10,16,1024]{3,2,1,0:T(8,128)S(1)} %copy-done.3, f32[16,16,1024]{2,1,0:T(8,128)S(1)} %copy-done.5, f32[5,16,1024]{2,1,0:T(8,128)S(1)} %get-tuple-element.25.coef_ref, f32[10,16,1024]{2,1,0:T(8,128)S(1)} %add.33.sum_ref, ...), custom_call_target="tpu_custom_call" | custom-call | tf_op jit(solution)/shard_map/segments/pallas_call | solution.py:317
  97.8 1.4 %head.1 = (f32[16,10,16,1024]{3,2,1,0:T(8,128)}, f32[16,1024]{1,0:T(8,128)S(1)}) custom-call(f32[16,10,16,1024]{3,2,1,0:T(8,128)S(1)} %segments.1.c_ref, f32[184,1024]{1,0:T(8,128)S(1)} %add.34.total_ref, f32[184,1024]{1,0:T(8,128)S(1)} %collective-permute-done.7.got_ref, f32[5,16,1024]{2,1,0:T(8,128)S(1)} %get-tuple-element.25.coef_ref, ...), custom_call_target="tpu_custom_call" | custom-call | tf_op jit(solution)/shard_map/head/pallas_call | solution.py:412
  99.2 4.0 %copy-done = f32[16,10,16,1024]{3,2,1,0:T(8,128)} copy-done((f32[16,10,16,1024]{3,2,1,0:T(8,128)}, f32[16,10,16,1024]{3,2,1,0:T(8,128)S(1)}, u32[]{:S(2)}) %copy-start) | copy-done | bytes 10485784
  103.2 1.7 %collective-permute-start.10 = (f32[16,1024]{1,0:T(8,128)S(1)}, f32[16,1024]{1,0:T(8,128)S(1)}, u32[]{:S(2)}, u32[]{:S(2)}) collective-permute-start(f32[16,1024]{1,0:T(8,128)S(1)} %get-tuple-element.31), channel_id=1, source_target_pairs={{0,8},{1,17},{2,10},{3,19},{4,12},{5,21},{6,14},{7,23},{8,0},{9,25... | collective-permute-start | bytes 196616 | tf_op jit(solution)/shard_map/ppermute | solution.py:35
  104.9 2.6 %collective-permute-done.10 = f32[16,1024]{1,0:T(8,128)S(1)} collective-permute-done((f32[16,1024]{1,0:T(8,128)S(1)}, f32[16,1024]{1,0:T(8,128)S(1)}, u32[]{:S(2)}, u32[]{:S(2)}) %collective-permute-start.10) | collective-permute-done | bytes 65568 | tf_op jit(solution)/shard_map/ppermute | solution.py:35
  107.5 1.8 %collective-permute-start.11 = (f32[16,1024]{1,0:T(8,128)S(1)}, f32[16,1024]{1,0:T(8,128)S(1)}, u32[]{:S(2)}, u32[]{:S(2)}) collective-permute-start(f32[16,1024]{1,0:T(8,128)S(1)} %add.35), channel_id=1, source_target_pairs={{0,16},{1,9},{2,18},{3,11},{4,20},{5,13},{6,22},{7,15},{8,24},{9,1... | collective-permute-start | bytes 196616 | tf_op jit(solution)/shard_map/ppermute | solution.py:35
  109.3 4.0 %copy-done.1 = f32[16,10,16,1024]{3,2,1,0:T(8,128)S(1)} copy-done((f32[16,10,16,1024]{3,2,1,0:T(8,128)S(1)}, f32[16,10,16,1024]{3,2,1,0:T(8,128)}, u32[]{:S(2)}) %copy-start.1) | copy-done | bytes 10485784
  113.3 1.1 copy-done.7
  114.4 1.1 copy-done.9
  115.5 0.9 copy-done.23
  116.4 6.8 %rest.1 = f32[16,10,16,1024]{3,2,1,0:T(8,128)} custom-call(f32[16,10,16,1024]{3,2,1,0:T(8,128)} %get-tuple-element.30.first_out_ref, f32[16,10,16,1024]{3,2,1,0:T(8,128)S(1)} %copy-done.1, f32[184,1024]{1,0:T(8,128)S(1)} %add.34.total_ref, f32[184,1024]{1,0:T(8,128)S(1)} %collective-permute-done.7.got_ref, ...), custom_call_target="tpu_custom_call", output_to_operand_aliasing={{}: (0, {})} | custom-call | tf_op jit(solution)/shard_map/rest/pallas_call | solution.py:422
  123.2 0.6 fusion.1
  (51 shorter events, 0.1 us)
Async XLA Ops:
  0.6 4.0 %copy-start.2 = (f32[16,10,16,1024]{3,2,1,0:T(8,128)S(1)}, f32[16,10,16,1024]{3,2,1,0:T(8,128)}, u32[]{:S(2)}) copy-start(f32[16,10,16,1024]{3,2,1,0:T(8,128)} %q_ref.3) | copy-start | bytes 31457284
  4.6 1.2 copy-start.4
  5.9 16.5 %copy-start.28 = (f32[16,256]{1,0:T(8,128)S(1)}, f32[16,256]{1,0:T(8,128)}, u32[]{:S(2)}) copy-start(f32[16,256]{1,0:T(8,128)} %param.11) | copy-start | bytes 49156
  5.9 16.5 %copy-start.29 = (f32[16,256]{1,0:T(8,128)S(1)}, f32[16,256]{1,0:T(8,128)}, u32[]{:S(2)}) copy-start(f32[16,256]{1,0:T(8,128)} %param.10) | copy-start | bytes 49156
  5.9 16.5 %copy-start.30 = (f32[16,256]{1,0:T(8,128)S(1)}, f32[16,256]{1,0:T(8,128)}, u32[]{:S(2)}) copy-start(f32[16,256]{1,0:T(8,128)} %param.9) | copy-start | bytes 49156
  5.9 29.8 %copy-start.5 = (f32[16,16,1024]{2,1,0:T(8,128)S(1)}, f32[16,16,1024]{2,1,0:T(8,128)}, u32[]{:S(2)}) copy-start(f32[16,16,1024]{2,1,0:T(8,128)} %w_ref.5) | copy-start | bytes 3145732
  5.9 29.8 %copy-start.26 = (f32[10]{0:T(128)S(1)}, f32[10]{0:T(128)}, u32[]{:S(2)}) copy-start(f32[10]{0:T(128)} %rate_ref.3) | copy-start | bytes 124
  5.9 29.8 %copy-start.27 = (f32[10]{0:T(128)S(1)}, f32[10]{0:T(128)}, u32[]{:S(2)}) copy-start(f32[10]{0:T(128)} %goal_ref.3) | copy-start | bytes 124
  13.8 0.8 copy-start.12
  14.7 0.8 copy-start.14
  15.5 0.8 copy-start.18
  16.3 0.8 copy-start.20
  17.2 0.6 copy-start.24
  17.8 17.9 %copy-start.16 = (f32[160,1024]{1,0:T(8,128)}, f32[160,1024]{1,0:T(8,128)S(1)}, u32[]{:S(2)}) copy-start(f32[160,1024]{1,0:T(8,128)S(1)} %get-tuple-element.21.lo_ref) | copy-start | bytes 1966084
  17.8 17.6 %collective-permute-start.2 = (f32[160,1024]{1,0:T(8,128)}, f32[160,1024]{1,0:T(8,128)S(1)}, u32[]{:S(2)}, u32[]{:S(2)}) collective-permute-start(f32[160,1024]{1,0:T(8,128)} %get-tuple-element.23.hi_ref), channel_id=1, source_target_pairs={{0,1},{1,2},{2,3},{3,4},{4,5},{5,6},{6,7},{7,0},{8,9},{9,10},{10,1... | collective-permute-start | bytes 1966088 | tf_op jit(solution)/shard_map/ppermute | solution.py:451
  18.3 17.4 %collective-permute-start.3 = (f32[160,1024]{1,0:T(8,128)S(1)}, f32[160,1024]{1,0:T(8,128)S(1)}, u32[]{:S(2)}, u32[]{:S(2)}) collective-permute-start(f32[160,1024]{1,0:T(8,128)S(1)} %get-tuple-element.21.lo_ref), channel_id=1, source_target_pairs={{0,7},{1,0},{2,1},{3,2},{4,3},{5,4},{6,5},{7,6},{8,15},{9,8},{10,9... | collective-permute-start | bytes 1966088 | tf_op jit(solution)/shard_map/ppermute | solution.py:452
  22.3 4.2 %collective-permute-start = (f32[1,3,16,256]{3,2,1,0:T(8,128)S(1)}, f32[1,3,16,256]{3,2,1,0:T(8,128)S(1)}, u32[]{:S(2)}, u32[]{:S(2)}) collective-permute-start(f32[1,3,16,256]{3,2,1,0:T(8,128)S(1)} %maximum_bitcast_fusion), channel_id=1, source_target_pairs={{0,8},{1,17},{2,10},{3,19},{4,12},{5,21},{6,14},{7,23},{8,0},{9,25... | collective-permute-start | bytes 147464 | tf_op jit(solution)/shard_map/ppermute | solution.py:35
  24.4 56.8 %copy-start.3 = (f32[16,10,16,1024]{3,2,1,0:T(8,128)S(1)}, f32[16,10,16,1024]{3,2,1,0:T(8,128)}, u32[]{:S(2)}) copy-start(f32[16,10,16,1024]{3,2,1,0:T(8,128)} %q_ref.3) | copy-start | bytes 31457284
  26.5 5.0 %collective-permute-start.1 = (f32[2,3,16,256]{3,2,1,0:T(8,128)S(1)}, f32[2,3,16,256]{3,2,1,0:T(8,128)S(1)}, u32[]{:S(2)}, u32[]{:S(2)}) collective-permute-start(f32[2,3,16,256]{3,2,1,0:T(8,128)S(1)} %pad_maximum_fusion.1), channel_id=1, source_target_pairs={{0,16},{1,9},{2,18},{3,11},{4,20},{5,13},{6,22},{7,15},{8,24},{9,1... | collective-permute-start | bytes 294920 | tf_op jit(solution)/shard_map/ppermute | solution.py:35
  35.7 13.0 %copy-start.10 = (f32[160,1024]{1,0:T(8,128)}, f32[160,1024]{1,0:T(8,128)S(1)}, u32[]{:S(2)}) copy-start(f32[160,1024]{1,0:T(8,128)S(1)} %collective-permute-done.3.above_ref) | copy-start | bytes 1966084
  35.7 1.3 %copy-start.13 = (f32[10,16,1024]{2,1,0:T(8,128)S(1)}, f32[10,16,1024]{2,1,0:T(8,128)}, u32[]{:S(2)}) copy-start(f32[10,16,1024]{2,1,0:T(8,128)} %copy-done.12) | copy-start | bytes 1966084
  37.0 1.1 copy-start.15
  38.1 1.1 copy-start.17
  39.2 1.1 copy-start.19
  40.3 1.1 copy-start.21
  41.4 0.8 copy-start.25
  46.2 51.5 %copy-start.22 = (f32[2,16,1024]{2,1,0:T(8,128)}, f32[2,16,1024]{2,1,0:T(8,128)S(1)}, u32[]{:S(2)}) copy-start(f32[2,16,1024]{2,1,0:T(8,128)S(1)} %get-tuple-element.27.edge_ref) | copy-start | bytes 393220
  46.2 11.9 %collective-permute-start.6 = (f32[184,1024]{1,0:T(8,128)S(1)}, f32[184,1024]{1,0:T(8,128)S(1)}, u32[]{:S(2)}, u32[]{:S(2)}) collective-permute-start(f32[184,1024]{1,0:T(8,128)S(1)} %get-tuple-element.26), channel_id=1, source_target_pairs={{0,8},{1,17},{2,10},{3,19},{4,12},{5,21},{6,14},{7,23},{8,0},{9,25... | collective-permute-start | bytes 2261000 | tf_op jit(solution)/shard_map/ppermute | solution.py:35
  48.6 19.9 %collective-permute-start.4 = (f32[10,16,1024]{2,1,0:T(8,128)}, f32[10,16,1024]{2,1,0:T(8,128)S(1)}, u32[]{:S(2)}, u32[]{:S(2)}) collective-permute-start(f32[10,16,1024]{2,1,0:T(8,128)} %get-tuple-element.17.sum_ref), channel_id=1, source_target_pairs={{0,8},{1,17},{2,10},{3,19},{4,12},{5,21},{6,14},{7,23},{8,0},{9,25... | collective-permute-start | bytes 1966088 | tf_op jit(solution)/shard_map/ppermute | solution.py:35
  58.3 39.5 %collective-permute-start.7 = (f32[184,1024]{1,0:T(8,128)S(1)}, f32[184,1024]{1,0:T(8,128)S(1)}, u32[]{:S(2)}, u32[]{:S(2)}) collective-permute-start(f32[184,1024]{1,0:T(8,128)S(1)} %add.34.total_ref), channel_id=1, source_target_pairs={{0,16},{1,9},{2,18},{3,11},{4,20},{5,13},{6,22},{7,15},{8,24},{9,1... | collective-permute-start | bytes 2261000 | tf_op jit(solution)/shard_map/ppermute | solution.py:35
  60.4 37.3 %collective-permute-start.8 = (f32[168,1024]{1,0:T(8,128)S(1)}, f32[168,1024]{1,0:T(8,128)S(1)}, u32[]{:S(2)}, u32[]{:S(2)}) collective-permute-start(f32[168,1024]{1,0:T(8,128)S(1)} %get-tuple-element.28), channel_id=1, source_target_pairs={{0,1},{1,2},{2,3},{3,4},{4,5},{5,6},{6,7},{7,0},{8,9},{9,10},{10,1... | collective-permute-start | bytes 2064392 | tf_op jit(solution)/shard_map/ppermute | solution.py:462
  60.8 36.9 %collective-permute-start.9 = (f32[168,1024]{1,0:T(8,128)S(1)}, f32[168,1024]{1,0:T(8,128)S(1)}, u32[]{:S(2)}, u32[]{:S(2)}) collective-permute-start(f32[168,1024]{1,0:T(8,128)S(1)} %get-tuple-element.29), channel_id=1, source_target_pairs={{0,7},{1,0},{2,1},{3,2},{4,3},{5,4},{6,5},{7,6},{8,15},{9,8},{10,9... | collective-permute-start | bytes 2064392 | tf_op jit(solution)/shard_map/ppermute | solution.py:463
  69.6 11.6 %collective-permute-start.5 = (f32[10,16,1024]{2,1,0:T(8,128)S(1)}, f32[10,16,1024]{2,1,0:T(8,128)S(1)}, u32[]{:S(2)}, u32[]{:S(2)}) collective-permute-start(f32[10,16,1024]{2,1,0:T(8,128)S(1)} %add.33.sum_ref), channel_id=1, source_target_pairs={{0,16},{1,9},{2,18},{3,11},{4,20},{5,13},{6,22},{7,15},{8,24},{9,1... | collective-permute-start | bytes 1966088 | tf_op jit(solution)/shard_map/ppermute | solution.py:35
  81.2 1.1 copy-start.11
  97.7 1.5 %copy-start.6 = (f32[168,1024]{1,0:T(8,128)}, f32[168,1024]{1,0:T(8,128)S(1)}, u32[]{:S(2)}) copy-start(f32[168,1024]{1,0:T(8,128)S(1)} %collective-permute-done.8.lo_ref) | copy-start | bytes 2064388
  97.7 5.5 %copy-start.8 = (f32[168,1024]{1,0:T(8,128)}, f32[168,1024]{1,0:T(8,128)S(1)}, u32[]{:S(2)}) copy-start(f32[168,1024]{1,0:T(8,128)S(1)} %collective-permute-done.9.hi_ref) | copy-start | bytes 2064388
  99.2 4.0 %copy-start = (f32[16,10,16,1024]{3,2,1,0:T(8,128)}, f32[16,10,16,1024]{3,2,1,0:T(8,128)S(1)}, u32[]{:S(2)}) copy-start(f32[16,10,16,1024]{3,2,1,0:T(8,128)S(1)} %segments.1.c_ref) | copy-start | bytes 31457284
  103.2 4.3 %collective-permute-start.10 = (f32[16,1024]{1,0:T(8,128)S(1)}, f32[16,1024]{1,0:T(8,128)S(1)}, u32[]{:S(2)}, u32[]{:S(2)}) collective-permute-start(f32[16,1024]{1,0:T(8,128)S(1)} %get-tuple-element.31), channel_id=1, source_target_pairs={{0,8},{1,17},{2,10},{3,19},{4,12},{5,21},{6,14},{7,23},{8,0},{9,25... | collective-permute-start | bytes 196616 | tf_op jit(solution)/shard_map/ppermute | solution.py:35
  107.5 15.7 %collective-permute-start.11 = (f32[16,1024]{1,0:T(8,128)S(1)}, f32[16,1024]{1,0:T(8,128)S(1)}, u32[]{:S(2)}, u32[]{:S(2)}) collective-permute-start(f32[16,1024]{1,0:T(8,128)S(1)} %add.35), channel_id=1, source_target_pairs={{0,16},{1,9},{2,18},{3,11},{4,20},{5,13},{6,22},{7,15},{8,24},{9,1... | collective-permute-start | bytes 196616 | tf_op jit(solution)/shard_map/ppermute | solution.py:35
  109.3 4.0 %copy-start.1 = (f32[16,10,16,1024]{3,2,1,0:T(8,128)S(1)}, f32[16,10,16,1024]{3,2,1,0:T(8,128)}, u32[]{:S(2)}) copy-start(f32[16,10,16,1024]{3,2,1,0:T(8,128)} %copy-done) | copy-start | bytes 31457284
  113.3 1.1 copy-start.7
  114.4 1.1 copy-start.9
  115.5 0.9 copy-start.23
